TPU v7x, 512 devices: a whole 4x4x16 slice. The times are simulated.
512 devices in a mesh: expert: 32 (over z_hi, x, core), row: 4 (over z_lo), col: 4 (over y).
Axes of the slice: x: 4, y: 4, z: 16 (z_hi: 4, z_lo: 4; z = z_hi * 4 + z_lo), core: 2. Of those that a mesh axis runs over, the one named last changes fastest.
Arguments:
- tokens: bfloat16 [32768, 3584], P(('expert', 'col'), 'row'), may hold values from -6 to 6
- slots: int32 [128, 6, 32, 2], P(('expert', 'col')), may hold values from 0 to 255
- counts: int32 [6, 32], replicated, may hold values from 1 to 256, as said below
- owner: int32 [32], replicated, may hold values from 0 to 31, each once
Outputs:
- moments: float32 [32, 3584, 3584], P('expert', 'row', 'col')
Inputs may be any that keep to these rules, and one draw needn't show every extreme that they name: `counts`: in every panel at least one expert's count is 256.
All inputs are finite; a program needn't handle non-finite values.
Results may differ from a plain program's by a relative error of at most 0.0003.
Values may be sent and summed in bfloat16 or wider, within the bound.
No kernel may reach another device: no remote copies, remote signals or barrier semaphores. Data moves between devices by JAX's collectives and lax.ppermute only.
A program may use at most 64 MiB of HBM per device.

v0:
```python
import jax
import jax.numpy as jnp
from jax import lax
from jax.sharding import PartitionSpec as P


def from_root(value, axis, root):
    mine = lax.axis_index(axis) == root
    return lax.psum(jnp.where(mine, value, jnp.zeros_like(value)), axis)


def panel_moment(outgoing):
    received = lax.all_to_all(outgoing, "expert", split_axis=1, concat_axis=1, tiled=True)
    panel_count = received.shape[0]
    feature_count = received.shape[3]
    left_rows = lax.all_gather(received, "col", axis=2, tiled=True)
    left_rows = left_rows.reshape(panel_count, -1, feature_count)
    right_rows = from_root(left_rows, "row", lax.axis_index("col"))
    return jnp.einsum("kpa,kpb->ab", left_rows, right_rows, preferred_element_type=jnp.float32)


def per_device(tokens, slots, counts, owner):
    col_count = lax.axis_size("col")
    slot_count = slots.shape[3]
    block_index = lax.axis_index("expert") * col_count + lax.axis_index("col")
    inverse = jnp.argsort(owner)
    dest_slots = jnp.take(slots[0], inverse, axis=1)
    dest_counts = jnp.take(counts, inverse, axis=1)
    position = block_index * slot_count + jnp.arange(slot_count, dtype=jnp.int32)
    usable = position[None, None, :] < dest_counts[:, :, None]
    picked = tokens[dest_slots]
    outgoing = jnp.where(usable[..., None], picked, jnp.zeros_like(picked))
    own_expert = inverse[lax.axis_index("expert")]
    row_total = jnp.sum(jnp.take(counts, own_expert, axis=1)).astype(jnp.float32)
    moment_tile = jnp.zeros((tokens.shape[1], tokens.shape[1]), jnp.float32)
    for panel in range(outgoing.shape[0]):
        moment_tile = moment_tile + panel_moment(outgoing[panel : panel + 1])
    return (moment_tile / row_total)[None]


def solution(mesh):
    return jax.shard_map(
        per_device,
        mesh=mesh,
        in_specs=(P(("expert", "col"), "row"), P(("expert", "col"), None, None, None), P(), P()),
        out_specs=P("expert", "row", "col"),
        check_vma=False,
    )
```

profile of v0, /device:TPU:1, one launch (start us, length us, event | category | flops | bytes accessed | tf_op | source)
XLA Modules:
  0.0 362.5 jit_solution(1238533840400708526)
XLA Ops:
  6.5 2.3 sort.17
  8.9 0.8 copy.21
  9.7 0.8 copy.22
  12.3 2.3 gather_fusion.2
  15.0 0.8 broadcast_select_fusion
  15.8 1.2 fusion.17
  17.0 35.4 %all_to_all.30 = bf16[1,32,2,896]{3,2,0,1:T(2,128)(2,1)S(1)} all-to-all(bf16[1,32,2,896]{3,2,0,1:T(2,128)(2,1)S(1)} %get-tuple-element.25), channel_id=1, replica_groups=mesh['expert'=32,'row'=4,'col'=4] {'expert'}, dimensions={1} | all-to-all | bytes 229376 | tf_op jit(solution)/shard_map/all_to_all | solution.py:13
  52.4 20.9 %all_to_all.31 = bf16[1,32,2,896]{3,2,0,1:T(2,128)(2,1)S(1)} all-to-all(bf16[1,32,2,896]{3,2,0,1:T(2,128)(2,1)S(1)} %get-tuple-element.26), channel_id=1, replica_groups=mesh['expert'=32,'row'=4,'col'=4] {'expert'}, dimensions={1} | all-to-all | bytes 229376 | tf_op jit(solution)/shard_map/all_to_all | solution.py:13
  73.3 20.9 %all_to_all.32 = bf16[1,32,2,896]{3,2,0,1:T(2,128)(2,1)S(1)} all-to-all(bf16[1,32,2,896]{3,2,0,1:T(2,128)(2,1)S(1)} %get-tuple-element.28), channel_id=1, replica_groups=mesh['expert'=32,'row'=4,'col'=4] {'expert'}, dimensions={1} | all-to-all | bytes 229376 | tf_op jit(solution)/shard_map/all_to_all | solution.py:13
  94.3 20.9 %all_to_all.33 = bf16[1,32,2,896]{3,2,0,1:T(2,128)(2,1)S(1)} all-to-all(bf16[1,32,2,896]{3,2,0,1:T(2,128)(2,1)S(1)} %get-tuple-element.29), channel_id=1, replica_groups=mesh['expert'=32,'row'=4,'col'=4] {'expert'}, dimensions={1} | all-to-all | bytes 229376 | tf_op jit(solution)/shard_map/all_to_all | solution.py:13
  115.2 5.1 %all-to-all-start.2 = ((bf16[1,32,2,896]{3,2,0,1:T(2,128)(2,1)}), bf16[1,32,2,896]{3,2,0,1:T(2,128)(2,1)S(1)}, u32[]{:S(2)}, u32[]{:S(2)}) async-start(bf16[1,32,2,896]{3,2,0,1:T(2,128)(2,1)} %get-tuple-element.27), calls=%async_computation.2 | async-start | bytes 229376 | tf_op jit(solution)/shard_map/all_to_all | solution.py:13
  120.4 11.2 %all_gather.18 = bf16[1,32,8,896]{3,1,0,2:T(8,128)(2,1)S(1)} all-gather(bf16[1,32,2,896]{3,1,0,2:T(8,128)(2,1)S(1)} %copy.25), channel_id=1, replica_groups=mesh['expert'=32,'row'=4,'col'=4] {'col'}, dimensions={2}, use_global_device_ids=true | all-gather | bytes 573440 | tf_op jit(solution)/shard_map/all_gather | solution.py:16
  131.6 10.0 %all_gather.19 = bf16[1,32,8,896]{3,1,0,2:T(8,128)(2,1)S(1)} all-gather(bf16[1,32,2,896]{3,1,0,2:T(8,128)(2,1)S(1)} %copy.28), channel_id=1, replica_groups=mesh['expert'=32,'row'=4,'col'=4] {'col'}, dimensions={2}, use_global_device_ids=true | all-gather | bytes 573440 | tf_op jit(solution)/shard_map/all_gather | solution.py:16
  141.7 19.5 %all-to-all-start.5 = ((bf16[1,32,2,896]{3,2,0,1:T(2,128)(2,1)}), bf16[1,32,2,896]{3,2,0,1:T(2,128)(2,1)S(1)}, u32[]{:S(2)}, u32[]{:S(2)}) async-start(bf16[1,32,2,896]{3,2,0,1:T(2,128)(2,1)} %get-tuple-element.24), calls=%async_computation.5 | async-start | bytes 229376 | tf_op jit(solution)/shard_map/all_to_all | solution.py:13
  161.2 10.8 %all_gather.20 = bf16[1,32,8,896]{3,1,0,2:T(8,128)(2,1)S(1)} all-gather(bf16[1,32,2,896]{3,1,0,2:T(8,128)(2,1)S(1)} %copy.31), channel_id=1, replica_groups=mesh['expert'=32,'row'=4,'col'=4] {'col'}, dimensions={2}, use_global_device_ids=true | all-gather | bytes 573440 | tf_op jit(solution)/shard_map/all_gather | solution.py:16
  172.1 10.0 %all_gather.21 = bf16[1,32,8,896]{3,1,0,2:T(8,128)(2,1)S(1)} all-gather(bf16[1,32,2,896]{3,1,0,2:T(8,128)(2,1)S(1)} %copy.34), channel_id=1, replica_groups=mesh['expert'=32,'row'=4,'col'=4] {'col'}, dimensions={2}, use_global_device_ids=true | all-gather | bytes 573440 | tf_op jit(solution)/shard_map/all_gather | solution.py:16
  182.1 10.6 %all_gather.22 = bf16[1,32,8,896]{3,1,0,2:T(8,128)(2,1)S(1)} all-gather(bf16[1,32,2,896]{3,1,0,2:T(8,128)(2,1)S(1)} %copy.37), channel_id=1, replica_groups=mesh['expert'=32,'row'=4,'col'=4] {'col'}, dimensions={2}, use_global_device_ids=true | all-gather | bytes 573440 | tf_op jit(solution)/shard_map/all_gather | solution.py:16
  192.7 10.8 %all_gather.23 = bf16[1,32,8,896]{3,1,0,2:T(8,128)(2,1)S(1)} all-gather(bf16[1,32,2,896]{3,1,0,2:T(8,128)(2,1)S(1)} %copy.40), channel_id=1, replica_groups=mesh['expert'=32,'row'=4,'col'=4] {'col'}, dimensions={2}, use_global_device_ids=true | all-gather | bytes 573440 | tf_op jit(solution)/shard_map/all_gather | solution.py:16
  203.6 1.0 select_bitcast_fusion
  204.5 0.9 select_bitcast_fusion.1
  205.5 1.0 select_bitcast_fusion.2
  206.4 0.9 select_bitcast_fusion.3
  207.3 0.9 select_bitcast_fusion.4
  208.3 1.0 select_bitcast_fusion.5
  211.8 0.7 select_reduce_fusion
  213.2 135.0 %all-reduce.3.cloned.1.call-done = (bf16[256,896]{1,0:T(8,128)(2,1)}, bf16[256,896]{1,0:T(8,128)(2,1)}, bf16[256,896]{1,0:T(8,128)(2,1)}, bf16[256,896]{1,0:T(8,...) async-done(((bf16[256,896]{1,0:T(8,128)(2,1)}, bf16[256,896]{1,0:T(8,128)(2,1)}, bf16[256,896]{1,0:T(8,128)(2,1)}, bf16[256,896]{1,0:T(8,128)(2,1)}, ...) | async-done | bytes 2752528 | tf_op jit(solution)/shard_map/psum | solution.py:9
  348.1 1.8 fusion.1
  349.9 0.7 fusion.3
  350.6 0.7 fusion.5
  351.3 0.7 fusion.9
  352.0 0.7 fusion.7
  352.7 2.9 divide_bitcast_fusion
  (39 shorter events, 3.0 us)
Async XLA Ops:
  6.5 5.8 %copy-start = (bf16[256,896]{1,0:T(8,128)(2,1)S(1)}, bf16[256,896]{1,0:T(8,128)(2,1)}, u32[]{:S(2)}) copy-start(bf16[256,896]{1,0:T(8,128)(2,1)} %param.4) | copy-start | bytes 1376260
  115.2 26.5 %all-to-all-start.2 = ((bf16[1,32,2,896]{3,2,0,1:T(2,128)(2,1)}), bf16[1,32,2,896]{3,2,0,1:T(2,128)(2,1)S(1)}, u32[]{:S(2)}, u32[]{:S(2)}) async-start(bf16[1,32,2,896]{3,2,0,1:T(2,128)(2,1)} %get-tuple-element.27), calls=%async_computation.2 | async-start | bytes 229376 | tf_op jit(solution)/shard_map/all_to_all | solution.py:13
  141.7 51.0 %all-to-all-start.5 = ((bf16[1,32,2,896]{3,2,0,1:T(2,128)(2,1)}), bf16[1,32,2,896]{3,2,0,1:T(2,128)(2,1)S(1)}, u32[]{:S(2)}, u32[]{:S(2)}) async-start(bf16[1,32,2,896]{3,2,0,1:T(2,128)(2,1)} %get-tuple-element.24), calls=%async_computation.5 | async-start | bytes 229376 | tf_op jit(solution)/shard_map/all_to_all | solution.py:13
  161.2 187.0 %all-reduce.3.cloned.1.call-start = ((), (), s32[]{:S(2)}) async-start(), calls=%async_computation.6 | async-start | bytes 5505024 | tf_op jit(solution)/shard_map/psum | solution.py:9
  205.5 6.3 %copy-start.6 = (s32[6,32]{1,0:T(8,128)S(1)}, s32[6,32]{1,0:T(8,128)}, u32[]{:S(2)}) copy-start(s32[6,32]{1,0:T(8,128)} %param.6) | copy-start | bytes 2308
  348.1 1.8 copy-start.5
  348.1 2.5 copy-start.4
  349.9 1.4 copy-start.3
  350.6 1.4 copy-start.2
  351.3 1.4 copy-start.1
Sparse Core Ops, SparseCore 0:
  209.4 138.7 all-reduce.2
where the time goes:
time: 363 us
  blocking collectives  162 us (45%)
  waiting for transfers between devices  135 us (37%)
  starting transfers between devices  24.6 us (7%)
  between operations  16.2 us (4%)
  other arithmetic  9.83 us (3%)
  local copies, waits for them, and re-layouts  7.67 us (2%)
  matrix products  7.42 us (2%)
    psum x1, waiting for transfers between devices, from_root(): return lax.psum(jnp.where(mine, value, jnp.zeros_like(value)), axis)  135 us
    all_to_all x4, blocking collectives, panel_moment(): lax.all_to_all(outgoing, 'expert', split_axis=1, concat_axis=1, tiled=True)  98.2 us
    all_gather x6, blocking collectives, panel_moment(): left_rows = lax.all_gather(received, 'col', axis=2, tiled=True)  63.5 us
    all_to_all x2, starting transfers between devices, panel_moment(): lax.all_to_all(outgoing, 'expert', split_axis=1, concat_axis=1, tiled=True)  24.6 us
    dot_general x6, matrix products, panel_moment(): jnp.einsum('kpa,kpb->ab', left_rows, right_rows, preferred_element_type=j...  7.42 us
  transfers between devices with their start and end apart: 3, of which 1 were waited for; matrix products, arithmetic and copies ran while one was open for 0% of the time, Pallas kernels for 0%

commit v1 on v0

--- a/solution.py
+++ b/solution.py
@@ -2,6 +2,13 @@
 import jax.numpy as jnp
 from jax import lax
 from jax.sharding import PartitionSpec as P
+
+
+def swapped_in(x, axis, dim):
+    size = lax.axis_size(axis)
+    pieces = jnp.stack([x for _ in range(size)])
+    pieces = lax.all_to_all(pieces, axis, split_axis=0, concat_axis=0)
+    return jnp.concatenate(pieces, axis=dim)
 
 
 def from_root(value, axis, root):
@@ -13,7 +20,7 @@
     received = lax.all_to_all(outgoing, "expert", split_axis=1, concat_axis=1, tiled=True)
     panel_count = received.shape[0]
     feature_count = received.shape[3]
-    left_rows = lax.all_gather(received, "col", axis=2, tiled=True)
+    left_rows = swapped_in(received, "col", 2)
     left_rows = left_rows.reshape(panel_count, -1, feature_count)
     right_rows = from_root(left_rows, "row", lax.axis_index("col"))
     return jnp.einsum("kpa,kpb->ab", left_rows, right_rows, preferred_element_type=jnp.float32)

time: 363 us -> 382 us (1.052)
  local copies, waits for them, and re-layouts: 7.67 us -> 38.3 us
  blocking collectives: 162 us -> 180 us
  starting transfers between devices: 24.6 us -> 7.15 us
  waiting for transfers between devices: 135 us -> 123 us
    all_gather x6 -> x0, blocking collectives: 63.5 us -> none  [panel_moment(): left_rows = lax.all_gather(received, 'col', axis=2, tiled=True)]
    all_to_all x4 -> x6, blocking collectives: 98.2 us -> 140 us  [panel_moment(): lax.all_to_all(outgoing, 'expert', split_axis=1, concat_axis=1, tiled=True)]
    all_to_all x0 -> x4, blocking collectives: none -> 39.8 us  [swapped_in(): pieces = lax.all_to_all(pieces, axis, split_axis=0, concat_axis=0)]
    another operation x0 -> x18, local copies, waits for them, and re-layouts: none -> 19.1 us
    psum x1, waiting for transfers between devices: 135 us -> 116 us  [from_root(): return lax.psum(jnp.where(mine, value, jnp.zeros_like(value)), axis)]
    all_to_all x2, starting transfers between devices: 24.6 us -> 6.93 us  [swapped_in(): pieces = lax.all_to_all(pieces, axis, split_axis=0, concat_axis=0)]
    select_n x0 -> x6, local copies, waits for them, and re-layouts: none -> 9.62 us  [from_root(): return lax.psum(jnp.where(mine, value, jnp.zeros_like(value)), axis)]
    all_to_all x2, waiting for transfers between devices: 0.01 us -> 6.54 us  [swapped_in(): pieces = lax.all_to_all(pieces, axis, split_axis=0, concat_axis=0)]
  transfers between devices with their start and end apart: 3 -> 3, of which waited for: 1 -> 2; matrix products, arithmetic and copies ran while one was open for 0% -> 6% of each run, Pallas kernels for 0% -> 0%
where the time goes in v1:
time: 382 us; the launch traced here: 380 us
  blocking collectives  180 us (47%)
  waiting for transfers between devices  123 us (32%)
  local copies, waits for them, and re-layouts  38.3 us (10%)
  between operations  16.3 us (4%)
  other arithmetic  8.69 us (2%)
  matrix products  7.28 us (2%)
  starting transfers between devices  7.15 us (2%)
    all_to_all x6, blocking collectives, panel_moment(): lax.all_to_all(outgoing, 'expert', split_axis=1, concat_axis=1, tiled=True)  140 us
    psum x1, waiting for transfers between devices, from_root(): return lax.psum(jnp.where(mine, value, jnp.zeros_like(value)), axis)  116 us
    all_to_all x4, blocking collectives, swapped_in(): pieces = lax.all_to_all(pieces, axis, split_axis=0, concat_axis=0)  39.8 us
    another operation x12, local copies, waits for them, and re-layouts  16.2 us
    select_n x6, local copies, waits for them, and re-layouts, from_root(): return lax.psum(jnp.where(mine, value, jnp.zeros_like(value)), axis)  9.62 us
  transfers between devices with their start and end apart: 3, of which 2 were waited for; matrix products, arithmetic and copies ran while one was open for 6% of the time, Pallas kernels for 0%

profile of v1, /device:TPU:1, one launch (start us, length us, event | category | flops | bytes accessed | tf_op | source)
XLA Modules:
  0.0 380.4 jit_solution(13951806302432291816)
XLA Ops:
  6.5 2.3 sort.17
  12.3 2.3 gather_fusion.2
  16.3 35.4 %all_to_all.78 = bf16[1,32,2,896]{3,2,0,1:T(2,128)(2,1)S(1)} all-to-all(bf16[1,32,2,896]{3,2,0,1:T(2,128)(2,1)S(1)} %get-tuple-element.24), channel_id=1, replica_groups=mesh['expert'=32,'row'=4,'col'=4] {'expert'}, dimensions={1} | all-to-all | bytes 229376 | tf_op jit(solution)/shard_map/all_to_all | solution.py:20
  51.8 20.9 %all_to_all.79 = bf16[1,32,2,896]{3,2,0,1:T(2,128)(2,1)S(1)} all-to-all(bf16[1,32,2,896]{3,2,0,1:T(2,128)(2,1)S(1)} %get-tuple-element.25), channel_id=1, replica_groups=mesh['expert'=32,'row'=4,'col'=4] {'expert'}, dimensions={1} | all-to-all | bytes 229376 | tf_op jit(solution)/shard_map/all_to_all | solution.py:20
  72.7 20.9 %all_to_all.80 = bf16[1,32,2,896]{3,2,0,1:T(2,128)(2,1)S(1)} all-to-all(bf16[1,32,2,896]{3,2,0,1:T(2,128)(2,1)S(1)} %get-tuple-element.26), channel_id=1, replica_groups=mesh['expert'=32,'row'=4,'col'=4] {'expert'}, dimensions={1} | all-to-all | bytes 229376 | tf_op jit(solution)/shard_map/all_to_all | solution.py:20
  93.6 20.9 %all_to_all.81 = bf16[1,32,2,896]{3,2,0,1:T(2,128)(2,1)S(1)} all-to-all(bf16[1,32,2,896]{3,2,0,1:T(2,128)(2,1)S(1)} %get-tuple-element.27), channel_id=1, replica_groups=mesh['expert'=32,'row'=4,'col'=4] {'expert'}, dimensions={1} | all-to-all | bytes 229376 | tf_op jit(solution)/shard_map/all_to_all | solution.py:20
  114.5 20.9 %all_to_all.82 = bf16[1,32,2,896]{3,2,0,1:T(2,128)(2,1)S(1)} all-to-all(bf16[1,32,2,896]{3,2,0,1:T(2,128)(2,1)S(1)} %get-tuple-element.28), channel_id=1, replica_groups=mesh['expert'=32,'row'=4,'col'=4] {'expert'}, dimensions={1} | all-to-all | bytes 229376 | tf_op jit(solution)/shard_map/all_to_all | solution.py:20
  135.5 20.9 %all_to_all.83 = bf16[1,32,2,896]{3,2,0,1:T(2,128)(2,1)S(1)} all-to-all(bf16[1,32,2,896]{3,2,0,1:T(2,128)(2,1)S(1)} %get-tuple-element.29), channel_id=1, replica_groups=mesh['expert'=32,'row'=4,'col'=4] {'expert'}, dimensions={1} | all-to-all | bytes 229376 | tf_op jit(solution)/shard_map/all_to_all | solution.py:20
  156.6 12.2 %all_to_all.84 = bf16[4,1,32,2,896]{4,3,2,1,0:T(2,128)(2,1)S(1)} all-to-all(bf16[4,1,32,2,896]{4,3,2,1,0:T(2,128)(2,1)S(1)} %stack.12), channel_id=1, replica_groups=mesh['expert'=32,'row'=4,'col'=4] {'col'}, dimensions={0} | all-to-all | bytes 917504 | tf_op jit(solution)/shard_map/all_to_all | solution.py:10
  169.0 9.7 %all_to_all.85 = bf16[4,1,32,2,896]{4,3,2,1,0:T(2,128)(2,1)S(1)} all-to-all(bf16[4,1,32,2,896]{4,3,2,1,0:T(2,128)(2,1)S(1)} %stack.13), channel_id=1, replica_groups=mesh['expert'=32,'row'=4,'col'=4] {'col'}, dimensions={0} | all-to-all | bytes 917504 | tf_op jit(solution)/shard_map/all_to_all | solution.py:10
  179.0 9.0 %all_to_all.86 = bf16[4,1,32,2,896]{4,3,2,1,0:T(2,128)(2,1)S(1)} all-to-all(bf16[4,1,32,2,896]{4,3,2,1,0:T(2,128)(2,1)S(1)} %stack.14), channel_id=1, replica_groups=mesh['expert'=32,'row'=4,'col'=4] {'col'}, dimensions={0} | all-to-all | bytes 917504 | tf_op jit(solution)/shard_map/all_to_all | solution.py:10
  188.2 9.0 %all_to_all.87 = bf16[4,1,32,2,896]{4,3,2,1,0:T(2,128)(2,1)S(1)} all-to-all(bf16[4,1,32,2,896]{4,3,2,1,0:T(2,128)(2,1)S(1)} %stack.16), channel_id=1, replica_groups=mesh['expert'=32,'row'=4,'col'=4] {'col'}, dimensions={0} | all-to-all | bytes 917504 | tf_op jit(solution)/shard_map/all_to_all | solution.py:10
  198.1 3.5 all-to-all-start.11
  201.6 6.5 %all-to-all-done.11 = bf16[4,1,32,2,896]{4,3,2,1,0:T(2,128)(2,1)S(1)} async-done(((bf16[4,1,32,2,896]{4,3,2,1,0:T(2,128)(2,1)}), bf16[4,1,32,2,896]{4,3,2,1,0:T(2,128)(2,1)S(1)}, u32[]{:S(2)}, u32[]{:S(2)}) %all-to-all-start.11) | async-done | bytes 458784 | tf_op jit(solution)/shard_map/all_to_all | solution.py:10
  209.2 3.5 all-to-all-start.7
  212.9 1.5 broadcast_select_fusion.1
  215.5 2.0 reshape.225
  217.4 2.1 copy.24
  219.5 2.0 reshape.222
  221.5 1.5 broadcast_select_fusion.5
  224.1 2.0 reshape.213
  226.1 1.5 broadcast_select_fusion.3
  227.6 1.1 copy.22
  228.7 2.0 reshape.219
  230.7 2.1 copy.20
  232.8 2.0 reshape.216
  234.8 2.1 copy.16
  236.9 2.0 reshape.210
  243.8 2.0 reshape.224
  249.9 116.3 %all-reduce.3.cloned.1.call-done = (bf16[256,896]{1,0:T(8,128)(2,1)}, bf16[256,896]{1,0:T(8,128)(2,1)}, bf16[256,896]{1,0:T(8,128)(2,1)}, bf16[256,896]{1,0:T(8,...) async-done(((bf16[256,896]{1,0:T(8,128)(2,1)}, bf16[256,896]{1,0:T(8,128)(2,1)}, bf16[256,896]{1,0:T(8,128)(2,1)}, bf16[256,896]{1,0:T(8,128)(2,1)}, ...) | async-done | bytes 2752528 | tf_op jit(solution)/shard_map/psum | solution.py:16
  366.2 1.8 fusion.5
  370.8 2.8 divide_bitcast_fusion
  (66 shorter events, 19.6 us)
Async XLA Ops:
  6.5 5.8 %copy-start = (bf16[256,896]{1,0:T(8,128)(2,1)S(1)}, bf16[256,896]{1,0:T(8,128)(2,1)}, u32[]{:S(2)}) copy-start(bf16[256,896]{1,0:T(8,128)(2,1)} %param.4) | copy-start | bytes 1376260
  198.1 10.0 %all-to-all-start.11 = ((bf16[4,1,32,2,896]{4,3,2,1,0:T(2,128)(2,1)}), bf16[4,1,32,2,896]{4,3,2,1,0:T(2,128)(2,1)S(1)}, u32[]{:S(2)}, u32[]{:S(2)}) async-start(bf16[4,1,32,2,896]{4,3,2,1,0:T(2,128)(2,1)} %stack.17), calls=%async_computation.11 | async-start | bytes 917504 | tf_op jit(solution)/shard_map/all_to_all | solution.py:10
  209.2 16.9 %all-to-all-start.7 = ((bf16[4,1,32,2,896]{4,3,2,1,0:T(2,128)(2,1)}), bf16[4,1,32,2,896]{4,3,2,1,0:T(2,128)(2,1)S(1)}, u32[]{:S(2)}, u32[]{:S(2)}) async-start(bf16[4,1,32,2,896]{4,3,2,1,0:T(2,128)(2,1)} %stack.15), calls=%async_computation.7 | async-start | bytes 917504 | tf_op jit(solution)/shard_map/all_to_all | solution.py:10
  212.6 153.5 %all-reduce.3.cloned.1.call-start = ((), (), s32[]{:S(2)}) async-start(), calls=%async_computation.12 | async-start | bytes 5505024 | tf_op jit(solution)/shard_map/psum | solution.py:16
  230.7 10.7 %copy-start.9 = (s32[6,32]{1,0:T(8,128)S(1)}, s32[6,32]{1,0:T(8,128)}, u32[]{:S(2)}) copy-start(s32[6,32]{1,0:T(8,128)} %param.6) | copy-start | bytes 2308
  247.4 118.8 %copy-start.2 = (bf16[256,896]{1,0:T(8,128)(2,1)S(1)}, bf16[256,896]{1,0:T(8,128)(2,1)}, u32[]{:S(2)}) copy-start(bf16[256,896]{1,0:T(8,128)(2,1)} %reshape.221) | copy-start | bytes 1376260
  366.2 1.8 copy-start.8
  366.2 2.5 copy-start.3
  366.2 2.5 copy-start.7
  368.0 1.4 copy-start.6
  368.7 1.4 copy-start.5
  369.4 1.4 copy-start.1
  369.4 1.4 copy-start.4
Sparse Core Ops, SparseCore 0:
  239.0 127.1 all-reduce.2
